TPU v7x, 512 devices: a whole 4x8x8 slice. The times are simulated.
512 devices in a mesh: dp: 64 (over y, z), mp: 8 (over x, core).
Axes of the slice: x: 4, y: 8, z: 8, core: 2. Of those that a mesh axis runs over, the one named last changes fastest.
Arguments:
- activations: bfloat16 [32768, 8192], P('dp', 'mp'), may hold values from -6 to 6
- out_grads: bfloat16 [32768, 8192], P('dp', 'mp'), may hold values from -0.09375 to 0.09375
- basis: bfloat16 [8192, 1024], P('mp'), may hold values from -0.0625 to 0.0625
- moment1: float32 [8192, 1024], P(('mp', 'dp')), may hold values from -1.5 to 1.5
- moment2: float32 [8192, 1024], P(('mp', 'dp')), may hold values from 0.0005 to 0.005
Outputs:
- new_first: float32 [8192, 1024], P(('mp', 'dp'))
- new_second: float32 [8192, 1024], P(('mp', 'dp'))
- update: bfloat16 [8, 1024, 8192], P(None, 'dp', 'mp')
All inputs are finite; a program needn't handle non-finite values.
Results may differ from a plain program's by a relative error of at most 0.0055.
Values may be sent and summed in bfloat16 or wider, within the bound.
A program may use at most 64 MiB of HBM per device.

v0:
```python
import jax
import jax.numpy as jnp
from jax import lax
from jax.sharding import Mesh
from jax.sharding import PartitionSpec as P

STEP = 100
DP = ("dp_0", "dp_1")
MP_DP = ("mp", "dp_0", "dp_1")


beta_first = 0.9
beta_second = 0.999
epsilon = 1e-08


def in_blocks(value, dim, peers):
    shape = value.shape
    parts = value.reshape(*shape[:dim], peers, shape[dim] // peers, *shape[dim + 1 :])
    return jnp.moveaxis(parts, dim, 0)


def sum_at_owner(value, axis, dim):
    parts = in_blocks(value, dim, lax.axis_size(axis))
    arrived = lax.all_to_all(parts, axis, split_axis=0, concat_axis=0, tiled=True)
    return arrived.sum(axis=0)


def joined_along(parts, dim):
    parts = jnp.moveaxis(parts, 0, dim)
    shape = parts.shape
    return parts.reshape(*shape[:dim], shape[dim] * shape[dim + 1], *shape[dim + 2 :])


def from_everyone(value, axis):
    peers = lax.axis_size(axis)
    return lax.all_to_all(
        jnp.broadcast_to(value[None], (peers, *value.shape)), axis, 0, 0, tiled=True
    )


def collect(value, axis, dim):
    return joined_along(from_everyone(value, axis), dim)


def sum_by_axis(total, axes):
    for axis in axes:
        total = lax.psum_scatter(total, axis, scatter_dimension=0, tiled=True)
    return total


def on_device(activations, out_grads, basis, moment1, moment2):
    partial_rank = jnp.dot(activations, basis, preferred_element_type=jnp.float32)
    shares = sum_at_owner(partial_rank, "mp", 1).astype(jnp.bfloat16)
    token_rank = collect(shares, "mp", 1)
    reduced = sum_by_axis(
        lax.dot_general(
            out_grads, token_rank, (((0,), (0,)), ((), ())), preferred_element_type=jnp.float32
        ),
        DP,
    )
    new_first = beta_first * moment1 + (1.0 - beta_first) * reduced
    new_second = beta_second * moment2 + (1.0 - beta_second) * reduced * reduced
    bias_first = 1.0 - beta_first**STEP
    bias_second = 1.0 - beta_second**STEP
    normed = (new_first / bias_first / (jnp.sqrt(new_second / bias_second) + epsilon)).astype(
        jnp.bfloat16
    )
    gathered = collect(normed[None], "mp", 0)
    groups, owned, ranks = gathered.shape
    stacked = gathered.reshape(groups * owned, ranks)
    full = lax.dot_general(
        stacked, basis, (((1,), (1,)), ((), ())), preferred_element_type=jnp.float32
    )
    update = full.astype(jnp.bfloat16).reshape(groups, owned, basis.shape[0])
    return (new_first, new_second, update)


def solution(mesh):
    finer = Mesh(mesh.devices.reshape(8, 8, mesh.shape["mp"]), ("dp_0", "dp_1", "mp"))
    in_specs = (P(DP, "mp"), P(DP, "mp"), P("mp", None), P(MP_DP, None), P(MP_DP, None))
    out_specs = (P(MP_DP, None), P(MP_DP, None), P(None, DP, "mp"))
    return jax.shard_map(
        on_device, mesh=finer, in_specs=in_specs, out_specs=out_specs, check_vma=False
    )
```

profile of v0, /device:TPU:1, one launch (start us, length us, event | category | flops | bytes accessed | tf_op | source)
XLA Modules:
  0.0 192.0 jit_solution(13038983599463154507)
XLA Ops:
  7.2 0.0 copy-start
  7.2 0.0 reduce-scatter.5.cloned.1.call-start
  7.2 1.5 copy-done
  8.8 2.5 %convolution_bitcast_fusion.1 = f32[64,8,8,128]{3,2,1,0:T(8,128)S(1)} fusion(bf16[512,1024]{1,0:T(8,128)(2,1)} %param.5, bf16[1024,1024]{1,0:T(8,128)(2,1)S(1)} %copy-done), kind=kOutput, calls=%fused_computation.2 | convolution fusion | flops 1073741824 | bytes 5242880 | tf_op jit(solution)/shard_map/dot_general | solution.py:53
  11.2 0.1 copy.43
  11.4 36.2 %all_to_all.15 = f32[8,512,128]{2,1,0:T(8,128)} all-to-all(f32[8,512,128]{2,1,0:T(8,128)S(1)} %bitcast.22), channel_id=1, replica_groups=mesh['dp_0'=8,'dp_1'=8,'mp'=8] {'mp'}, dimensions={0} | all-to-all | bytes 4194304 | tf_op jit(solution)/shard_map/all_to_all | solution.py:25
  47.5 1.7 reduce_sum.9
  49.2 0.0 copy-start.3
  49.3 0.1 copy.34
  49.4 0.1 broadcast_in_dim.4
  49.5 18.5 %all_to_all.16 = bf16[8,512,128]{1,2,0:T(8,128)(2,1)S(1)} all-to-all(bf16[8,512,128]{1,2,0:T(8,128)(2,1)S(1)} %broadcast_in_dim.4), channel_id=1, replica_groups=mesh['dp_0'=8,'dp_1'=8,'mp'=8] {'mp'}, dimensions={0} | all-to-all | bytes 2097152 | tf_op jit(solution)/shard_map/all_to_all | solution.py:37
  68.0 0.0 copy-done.3
  68.0 3.2 %convolution_bitcast_fusion = f32[1024,1024]{0,1:T(8,128)} fusion(bf16[512,1024]{0,1:T(8,128)(2,1)S(1)} %bitcast.24, bf16[512,1024]{1,0:T(8,128)(2,1)S(1)} %copy-done.3), kind=kOutput, calls=%fused_computation | convolution fusion | flops 1073741824 | bytes 6291456 | tf_op jit(solution)/shard_map/dot_general | solution.py:57
  71.2 0.0 copy-start.1
  71.2 0.0 copy-start.2
  71.2 0.0 reduce-scatter.5.cloned.1.call-update
  71.2 0.0 reduce-scatter.7.cloned.1.call-start
  71.3 56.6 %reduce-scatter.5.cloned.1.call-done = f32[128,1024]{0,1:T(8,128)} async-done(((f32[1024,1024]{0,1:T(8,128)}), f32[128,1024]{0,1:T(8,128)}) %reduce-scatter.5.cloned.1.call-update) | async-done | bytes 524304 | tf_op jit(solution)/shard_map/reduce_scatter | solution.py:48
  127.8 2.0 %copy.38 = f32[128,1024]{1,0:T(8,128)} copy(f32[128,1024]{0,1:T(8,128)} %reduce-scatter.5.cloned.1.call-done) | data formatting | bytes 1048576
  129.9 0.0 reduce-scatter.7.cloned.1.call-update
  129.9 36.2 %reduce-scatter.7.cloned.1.call-done = f32[16,1024]{1,0:T(8,128)} async-done(((f32[128,1024]{1,0:T(8,128)}), f32[16,1024]{1,0:T(8,128)}) %reduce-scatter.7.cloned.1.call-update) | async-done | bytes 65552 | tf_op jit(solution)/shard_map/reduce_scatter | solution.py:48
  166.1 0.0 copy-done.1
  166.1 0.0 copy-done.2
  166.1 1.5 divide_convert_fusion
  167.6 16.0 %all_to_all.17 = bf16[8,1,16,1024]{3,2,1,0:T(8,128)(2,1)S(1)} all-to-all(bf16[8,1,16,1024]{3,2,1,0:T(8,128)(2,1)S(1)} %broadcast_in_dim.5), channel_id=1, replica_groups=mesh['dp_0'=8,'dp_1'=8,'mp'=8] {'mp'}, dimensions={0} | all-to-all | bytes 524288 | tf_op jit(solution)/shard_map/all_to_all | solution.py:37
  183.7 1.5 convolution_convert_fusion
  (1 shorter events, 0.0 us)
Async XLA Ops:
  7.2 1.6 copy-start
  7.2 120.7 %reduce-scatter.5.cloned.1.call-start = ((), (), s32[]{:S(2)}) async-start(), calls=%async_computation.5 | async-start | bytes 4718592 | tf_op jit(solution)/shard_map/reduce_scatter | solution.py:48
  49.2 18.8 %copy-start.3 = (bf16[512,1024]{1,0:T(8,128)(2,1)S(1)}, bf16[512,1024]{1,0:T(8,128)(2,1)}, u32[]{:S(2)}) copy-start(bf16[512,1024]{1,0:T(8,128)(2,1)} %param.6) | copy-start | bytes 3145732
  71.2 94.9 %copy-start.1 = (f32[16,1024]{1,0:T(8,128)S(1)}, f32[16,1024]{1,0:T(8,128)}, u32[]{:S(2)}) copy-start(f32[16,1024]{1,0:T(8,128)} %param.9) | copy-start | bytes 196612
  71.2 94.9 %copy-start.2 = (f32[16,1024]{1,0:T(8,128)S(1)}, f32[16,1024]{1,0:T(8,128)}, u32[]{:S(2)}) copy-start(f32[16,1024]{1,0:T(8,128)} %param.8) | copy-start | bytes 196612
  71.2 94.9 %reduce-scatter.7.cloned.1.call-start = ((), (), s32[]{:S(2)}) async-start(), calls=%async_computation.6 | async-start | bytes 589824 | tf_op jit(solution)/shard_map/reduce_scatter | solution.py:48
Sparse Core Ops, SparseCore 0:
  71.4 56.4 reduce-scatter.4
  130.6 35.4 reduce-scatter.6
where the time goes:
time: 192 us
  waiting for transfers between devices  92.8 us (48%)
  blocking collectives  70.7 us (37%)
  between operations  14.1 us (7%)
  matrix products  7.21 us (4%)
  local copies, waits for them, and re-layouts  3.94 us (2%)
  other arithmetic  3.22 us (2%)
    reduce_scatter x2, waiting for transfers between devices, sum_by_axis(): total = lax.psum_scatter(total, axis, scatter_dimension=0, tiled=True)  92.8 us
    all_to_all x1, blocking collectives, sum_at_owner(): lax.all_to_all(parts, axis, split_axis=0, concat_axis=0, tiled=True)  36.2 us
    all_to_all x2, blocking collectives, from_everyone(): lax.all_to_all(jnp.broadcast_to(value[None], (peers, *value.shape)), axis...  34.6 us
  transfers between devices with their start and end apart: 2, of which 2 were waited for; matrix products, arithmetic and copies ran while one was open for 0% of the time, Pallas kernels for 0%

commit v1 on v0

v1 whole, which is shorter than its diff:
```python
import jax
import jax.numpy as jnp
from jax import lax
from jax.experimental import pallas as pl
from jax.experimental.pallas import tpu as pltpu
from jax.sharding import Mesh
from jax.sharding import PartitionSpec as P

STEP = 100
beta_first = 0.9
beta_second = 0.999
epsilon = 1e-08

DEVICE = pl.DeviceIdType.MESH
SIZES = {"y": 8, "z": 8, "x": 4, "c": 2}
TOKENS, FEATURES, OUTS, RANK = 512, 1024, 1024, 1024
CHUNKS = 4
WIDE = RANK // CHUNKS
HALF = TOKENS // 2
SHARE = TOKENS // 8
OWNED = 16

STAGE_AT = (0.0, 1.3, 4.0, 6.8, 8.2, 13.0, 17.5, 21.0)
STAGE_GAP = (0.1, 1.0, 1.0, 1.4, 1.8, 3.0, 3.0, 3.0)


def f32(value):
    return value.astype(jnp.float32)


def bf16(value):
    return value.astype(jnp.bfloat16)


def kernel(
    a_hbm, g_hbm, b_hbm, m1_hbm, m2_hbm,
    first_out, second_out, update_out,
    a_v, g_v, b_v, m1_v, m2_v, gt_v,
    p_v, r0_v, q_v, r1_v, t_v, r_v, s0_v, s_v, u_v, n_v, full_v,
    load_sem, pair_s, pair_r, rs_s, rs_r, ag_s, ag_r, join_s, join_r,
    one_s, one_r, two_s, two_r, norm_s, norm_r,
):
    at = {axis: lax.axis_index(axis) for axis in SIZES}
    x, c = at["x"], at["c"]

    def shifted(axis, offset):
        return lax.rem(at[axis] + offset, SIZES[axis])

    def columns(k):
        return pl.ds(k * WIDE, WIDE)

    def load(src, dst, index):
        copy = pltpu.make_async_copy(src, dst, load_sem.at[index])
        copy.start()
        return copy

    load_a = load(a_hbm, a_v, 0)
    load_b = [load(b_hbm.at[:, columns(k)], b_v.at[:, columns(k)], 1 + k) for k in range(CHUNKS)]
    load_g = load(g_hbm, g_v, 1 + CHUNKS)
    load_m1 = load(m1_hbm, m1_v, 2 + CHUNKS)
    load_m2 = load(m2_hbm, m2_v, 3 + CHUNKS)

    mp_peers = [
        {"x": shifted("x", dx), "c": shifted("c", dc)} for dx in range(4) for dc in range(2) if dx or dc
    ]
    barrier = pltpu.get_barrier_semaphore()
    peers = mp_peers + [{axis: shifted(axis, o)} for axis in ("y", "z") for o in range(1, 8)]
    for peer in peers:
        pl.semaphore_signal(barrier, inc=1, device_id=peer, device_id_type=DEVICE)

    sent = []
    coming = {}

    def send(src, dst, sems, slot, peer, tag):
        copy = pltpu.make_async_remote_copy(
            src_ref=src, dst_ref=dst, send_sem=sems[0].at[slot], recv_sem=sems[1].at[slot],
            device_id=peer, device_id_type=DEVICE,
        )
        copy.start()
        sent.append(copy)
        coming.setdefault(tag, []).append(copy)

    def arrive(tag):
        for copy in coming[tag]:
            copy.wait_recv()

    def axes_of(k):
        return ("y", "z") if k % 2 == 0 else ("z", "y")

    def project(k):
        load_b[k].wait()
        p_v[k] = bf16(jnp.dot(a_v[...], b_v[:, columns(k)], preferred_element_type=jnp.float32))
        if k == 0:
            pl.semaphore_wait(barrier, len(peers))
        send(
            p_v.at[k, pl.ds(pl.multiple_of((1 - c) * HALF, HALF), HALF)], r0_v.at[k],
            (pair_s, pair_r), k, {"c": 1 - c}, (0, k),
        )

    def pair_sum(k):
        arrive((0, k))
        mine = p_v[k, pl.ds(pl.multiple_of(c * HALF, HALF), HALF)]
        q_v[k] = bf16(f32(mine) + f32(r0_v[k]))
        for o in (2, 1, 3):
            to = shifted("x", o)
            send(
                q_v.at[k, pl.ds(pl.multiple_of(to * SHARE, SHARE), SHARE)], r1_v.at[k, o - 1],
                (rs_s, rs_r), 3 * k + o - 1, {"x": to}, (1, k),
            )

    def own_rows():
        return pl.ds(pl.multiple_of(c * HALF + x * SHARE, SHARE), SHARE)

    def token_share(k):
        arrive((1, k))
        total = f32(q_v[k, pl.ds(pl.multiple_of(x * SHARE, SHARE), SHARE)])
        for o in range(3):
            total = total + f32(r1_v[k, o])
        t_v[k, own_rows()] = bf16(total)
        for o in (2, 1, 3):
            send(
                t_v.at[k, own_rows()], t_v.at[k, own_rows()],
                (ag_s, ag_r), 3 * k + o - 1, {"x": shifted("x", o)}, (2, k),
            )

    def join(k):
        arrive((2, k))
        rows = pl.ds(pl.multiple_of(c * HALF, HALF), HALF)
        send(t_v.at[k, rows], t_v.at[k, rows], (join_s, join_r), k, {"c": 1 - c}, (3, k))

    def gradient(k):
        arrive((3, k))
        total = bf16(jnp.dot(gt_v[...], t_v[k], preferred_element_type=jnp.float32))
        if k % 2 == 0:
            r_v[k] = total.reshape(8, 128, WIDE)
        else:
            for y in range(8):
                r_v[k, :, pl.ds(16 * y, 16)] = total[128 * y : 128 * y + 128].reshape(8, 16, WIDE)
        axis = axes_of(k)[0]
        for o in (4, 3, 5, 2, 6, 1, 7):
            to = shifted(axis, o)
            send(r_v.at[k, to], s0_v.at[k, o - 1], (one_s, one_r), 7 * k + o - 1, {axis: to}, (4, k))

    def first_sum(k):
        arrive((4, k))
        total = f32(r_v[k, at[axes_of(k)[0]]])
        for o in range(7):
            total = total + f32(s0_v[k, o])
        s_v[k] = bf16(total).reshape(8, OWNED, WIDE)
        axis = axes_of(k)[1]
        for o in (4, 3, 5, 2, 6, 1, 7):
            to = shifted(axis, o)
            send(s_v.at[k, to], u_v.at[k, o - 1], (two_s, two_r), 7 * k + o - 1, {axis: to}, (5, k))

    def moments(k):
        arrive((5, k))
        reduced = f32(s_v[k, at[axes_of(k)[1]]])
        for o in range(7):
            reduced = reduced + f32(u_v[k, o])
        new_first = beta_first * m1_v[:, columns(k)] + (1.0 - beta_first) * reduced
        new_second = beta_second * m2_v[:, columns(k)] + (1.0 - beta_second) * reduced * reduced
        first_out[:, columns(k)] = new_first
        second_out[:, columns(k)] = new_second
        bias_first = 1.0 - beta_first**STEP
        bias_second = 1.0 - beta_second**STEP
        normed = new_first / bias_first / (jnp.sqrt(new_second / bias_second) + epsilon)
        me = 2 * x + c
        n_v[k, me] = bf16(normed)
        for i, peer in enumerate(mp_peers):
            send(n_v.at[k, me], n_v.at[k, me], (norm_s, norm_r), 7 * k + i, peer, (6, k))

    def expand(k):
        arrive((6, k))
        stacked = n_v[k].reshape(8 * OWNED, WIDE)
        part = lax.dot_general(
            stacked, b_v[:, columns(k)], (((1,), (1,)), ((), ())), preferred_element_type=jnp.float32
        )
        if k == 0:
            full_v[...] = part
        elif k < CHUNKS - 1:
            full_v[...] += part
        else:
            update_out[...] = bf16(full_v[...] + part).reshape(8, OWNED, FEATURES)

    stages = (project, pair_sum, token_share, join, gradient, first_sum, moments, expand)
    plan = sorted(
        (STAGE_AT[s] + k * STAGE_GAP[s], s, k) for s in range(len(stages)) for k in range(CHUNKS)
    )
    load_a.wait()
    turned = False
    for _, s, k in plan:
        if s == 1 and not turned:
            load_g.wait()
            gt_v[...] = g_v[...].T
            load_m1.wait()
            load_m2.wait()
            turned = True
        stages[s](k)
    for copy in sent:
        copy.wait_send()


def on_device(activations, out_grads, basis, moment1, moment2):
    def vmem(*shape, dtype=jnp.bfloat16):
        return pltpu.VMEM(shape, dtype)

    sems = pltpu.SemaphoreType.DMA
    n = CHUNKS
    pairs = [sems((count * n,)) for count in (1, 3, 3, 1, 7, 7, 7) for _ in range(2)]
    anywhere = pl.BlockSpec(memory_space=pl.ANY)
    in_vmem = pl.BlockSpec(memory_space=pltpu.VMEM)
    return pl.pallas_call(
        kernel,
        out_shape=(
            jax.ShapeDtypeStruct((OWNED, RANK), jnp.float32),
            jax.ShapeDtypeStruct((OWNED, RANK), jnp.float32),
            jax.ShapeDtypeStruct((8, OWNED, FEATURES), jnp.bfloat16),
        ),
        in_specs=[anywhere] * 5,
        out_specs=(in_vmem,) * 3,
        scratch_shapes=[
            vmem(TOKENS, FEATURES),
            vmem(TOKENS, OUTS),
            vmem(FEATURES, RANK),
            vmem(OWNED, RANK, dtype=jnp.float32),
            vmem(OWNED, RANK, dtype=jnp.float32),
            vmem(OUTS, TOKENS),
            vmem(n, TOKENS, WIDE),
            vmem(n, HALF, WIDE),
            vmem(n, HALF, WIDE),
            vmem(n, 3, SHARE, WIDE),
            vmem(n, TOKENS, WIDE),
            vmem(n, 8, 128, WIDE),
            vmem(n, 7, 128, WIDE),
            vmem(n, 8, OWNED, WIDE),
            vmem(n, 7, OWNED, WIDE),
            vmem(n, 8, OWNED, WIDE),
            vmem(8 * OWNED, FEATURES, dtype=jnp.float32),
            sems((4 + n,)),
        ]
        + pairs,
        compiler_params=pltpu.CompilerParams(
            collective_id=0, has_side_effects=True, vmem_limit_bytes=40 * 1024 * 1024
        ),
        name="projected_adam",
    )(activations, out_grads, basis, moment1, moment2)


def solution(mesh):
    finer = Mesh(mesh.devices.reshape(8, 8, 4, 2), ("y", "z", "x", "c"))
    dp, mp, owners = ("y", "z"), ("x", "c"), ("x", "c", "y", "z")
    in_specs = (P(dp, mp), P(dp, mp), P(mp, None), P(owners, None), P(owners, None))
    out_specs = (P(owners, None), P(owners, None), P(None, dp, mp))
    return jax.shard_map(
        on_device, mesh=finer, in_specs=in_specs, out_specs=out_specs, check_vma=False
    )
```

time: 192 us -> 78.8 us (0.41)
  waiting for transfers between devices: 92.8 us -> 0 us
  blocking collectives: 70.7 us -> 0 us
  Pallas kernels: 0 us -> 70.1 us
  between operations: 14.1 us -> 0.65 us
  matrix products: 7.21 us -> 0 us
  local copies, waits for them, and re-layouts: 3.94 us -> 7.67 us
  other arithmetic: 3.22 us -> 0 us
    reduce_scatter x2 -> x0, waiting for transfers between devices: 92.8 us -> none  [sum_by_axis(): total = lax.psum_scatter(total, axis, scatter_dimension=0, tiled=True)]
    all_to_all x3 -> x0, blocking collectives: 70.7 us -> none  [the longest x1 36.2 us: sum_at_owner(): lax.all_to_all(parts, axis, split_axis=0, concat_axis=0, tiled=True)]
    pallas_call x0 -> x1, Pallas kernels: none -> 70.1 us  [on_device(): pl.pallas_call(kernel, out_shape=(jax.ShapeDtypeStruct((OWNED, RANK), jnp...]
    dot_general x3 -> x0, matrix products: 7.21 us -> none  [the longest x1 3.21 us: on_device(): lax.dot_general(out_grads, token_rank, (((0,), (0,)), ((), ())), preferre...]
    unnamed x9 -> x13, local copies, waits for them, and re-layouts: 3.59 us -> 7.67 us
  transfers between devices with their start and end apart: 2 -> 0, of which waited for: 2 -> 0; matrix products, arithmetic and copies ran while one was open for 0% -> 0% of each run, Pallas kernels for 0% -> 0%
where the time goes in v1:
time: 78.8 us; the launch traced here: 78.5 us
  Pallas kernels  70.1 us (89%)
  local copies, waits for them, and re-layouts  7.67 us (10%)
    pallas_call x1, Pallas kernels, on_device(): pl.pallas_call(kernel, out_shape=(jax.ShapeDtypeStruct((OWNED, RANK), jnp...  70.1 us
    unnamed x13, local copies, waits for them, and re-layouts  7.67 us

profile of v1, /device:TPU:1, one launch (start us, length us, event | category | flops | bytes accessed | tf_op | source)
XLA Modules:
  0.0 78.5 jit_solution(8495882083271371843)
XLA Ops:
  0.6 0.0 copy-start
  0.6 1.6 %copy-done = bf16[1024,1024]{1,0:T(8,128)(2,1)S(1)} copy-done((bf16[1024,1024]{1,0:T(8,128)(2,1)S(1)}, bf16[1024,1024]{1,0:T(8,128)(2,1)}, u32[]{:S(2)}) %copy-start) | copy-done | bytes 2097176
  2.2 0.0 copy-start.1
  2.2 1.2 %copy-done.1 = bf16[512,1024]{1,0:T(8,128)(2,1)S(1)} copy-done((bf16[512,1024]{1,0:T(8,128)(2,1)S(1)}, bf16[512,1024]{1,0:T(8,128)(2,1)}, u32[]{:S(2)}) %copy-start.1) | copy-done | bytes 1048600
  3.4 0.0 copy-start.2
  3.5 1.2 %copy-done.2 = bf16[512,1024]{1,0:T(8,128)(2,1)S(1)} copy-done((bf16[512,1024]{1,0:T(8,128)(2,1)S(1)}, bf16[512,1024]{1,0:T(8,128)(2,1)}, u32[]{:S(2)}) %copy-start.2) | copy-done | bytes 1048600
  4.7 0.0 copy-start.3
  4.7 0.8 %copy-done.3 = f32[16,1024]{1,0:T(8,128)S(1)} copy-done((f32[16,1024]{1,0:T(8,128)S(1)}, f32[16,1024]{1,0:T(8,128)}, u32[]{:S(2)}) %copy-start.3) | copy-done | bytes 65560
  5.5 0.0 copy-start.4
  5.5 0.8 %copy-done.4 = f32[16,1024]{1,0:T(8,128)S(1)} copy-done((f32[16,1024]{1,0:T(8,128)S(1)}, f32[16,1024]{1,0:T(8,128)}, u32[]{:S(2)}) %copy-start.4) | copy-done | bytes 65560
  6.4 70.1 %projected_adam.1 = (f32[16,1024]{1,0:T(8,128)S(1)}, f32[16,1024]{1,0:T(8,128)S(1)}, bf16[8,16,1024]{2,1,0:T(8,128)(2,1)S(1)}) custom-call(bf16[512,1024]{1,0:T(8,128)(2,1)S(1)} %copy-done.1, bf16[512,1024]{1,0:T(8,128)(2,1)S(1)} %copy-done.2, bf16[1024,1024]{1,0:T(8,128)(2,1)S(1)} %copy-done, f32[16,1024]{1,0:T(8,128)S(1)} %copy-done.3, ...), custom_call_target="tpu_custom_call" | custom-call | tf_op jit(solution)/shard_map/projected_adam/pallas_call | solution.py:212
  76.5 0.6 copy.11
  77.1 0.6 copy.12
  77.8 0.7 copy.13
Async XLA Ops:
  0.6 1.6 %copy-start = (bf16[1024,1024]{1,0:T(8,128)(2,1)S(1)}, bf16[1024,1024]{1,0:T(8,128)(2,1)}, u32[]{:S(2)}) copy-start(bf16[1024,1024]{1,0:T(8,128)(2,1)} %b_hbm.1) | copy-start | bytes 6291460
  2.2 1.2 %copy-start.1 = (bf16[512,1024]{1,0:T(8,128)(2,1)S(1)}, bf16[512,1024]{1,0:T(8,128)(2,1)}, u32[]{:S(2)}) copy-start(bf16[512,1024]{1,0:T(8,128)(2,1)} %a_hbm.1) | copy-start | bytes 3145732
  3.4 1.2 %copy-start.2 = (bf16[512,1024]{1,0:T(8,128)(2,1)S(1)}, bf16[512,1024]{1,0:T(8,128)(2,1)}, u32[]{:S(2)}) copy-start(bf16[512,1024]{1,0:T(8,128)(2,1)} %g_hbm.1) | copy-start | bytes 3145732
  4.7 0.8 %copy-start.3 = (f32[16,1024]{1,0:T(8,128)S(1)}, f32[16,1024]{1,0:T(8,128)}, u32[]{:S(2)}) copy-start(f32[16,1024]{1,0:T(8,128)} %m1_hbm.1) | copy-start | bytes 196612
  5.5 0.8 %copy-start.4 = (f32[16,1024]{1,0:T(8,128)S(1)}, f32[16,1024]{1,0:T(8,128)}, u32[]{:S(2)}) copy-start(f32[16,1024]{1,0:T(8,128)} %m2_hbm.1) | copy-start | bytes 196612

commit v2 on v1

v2 whole, which is shorter than its diff:
```python
import jax
import jax.numpy as jnp
from jax import lax
from jax.experimental import pallas as pl
from jax.experimental.pallas import tpu as pltpu
from jax.sharding import Mesh
from jax.sharding import PartitionSpec as P

STEP = 100
beta_first = 0.9
beta_second = 0.999
epsilon = 1e-08

DEVICE = pl.DeviceIdType.MESH
SIZES = {"y": 8, "z": 8, "x": 4, "c": 2}
TOKENS, FEATURES, OUTS, RANK = 512, 1024, 1024, 1024
CHUNKS = 2
SPLIT = 2
WIDE = RANK // CHUNKS
PART = WIDE // SPLIT
PARTS = CHUNKS * SPLIT
HALF = TOKENS // 2
SHARE = TOKENS // 8
OWNED = 16

STAGE_AT = (0.0, 2.2, 7.5, 13.0, 15.5, 21.0, 28.0, 33.0, 37.0)
STAGE_GAP = (1.4, 1.6, 2.8, 2.8, 2.8, 3.0, 3.0, 3.0, 3.0)


def f32(value):
    return value.astype(jnp.float32)


def bf16(value):
    return value.astype(jnp.bfloat16)


def kernel(
    a_hbm, g_hbm, b_hbm, m1_hbm, m2_hbm,
    first_out, second_out, update_out,
    a_v, g_v, b_v, m1_v, m2_v, gt_v,
    p_v, p32_v, r0_v, q_v, q32_v, r1_v, t_v, r_v, r32_v, hop_v, in_v, end_v,
    s_v, s32_v, u_v, n_v, full_v,
    load_sem, send_sem, pair_r, rs_r, ag_r, join_r, in_r, end_r, two_r, norm_r,
):
    at = {axis: lax.axis_index(axis) for axis in SIZES}
    x, c = at["x"], at["c"]

    def shifted(axis, offset):
        return lax.rem(at[axis] + offset + SIZES[axis], SIZES[axis])

    def columns(k):
        return pl.ds(k * WIDE, WIDE)

    def load(src, dst, index):
        copy = pltpu.make_async_copy(src, dst, load_sem.at[index])
        copy.start()
        return copy

    load_a = load(a_hbm, a_v, 0)
    load_b = [load(b_hbm.at[:, columns(k)], b_v.at[:, columns(k)], 1 + k) for k in range(CHUNKS)]
    load_g = load(g_hbm, g_v, 1 + CHUNKS)
    load_m1 = load(m1_hbm, m1_v, 2 + CHUNKS)
    load_m2 = load(m2_hbm, m2_v, 3 + CHUNKS)

    mp_peers = [
        {"x": shifted("x", dx), "c": shifted("c", dc)} for dx in range(4) for dc in range(2) if dx or dc
    ]
    barrier = pltpu.get_barrier_semaphore()
    peers = mp_peers + [{axis: shifted(axis, o)} for axis in ("y", "z") for o in range(1, 8)]
    for peer in peers:
        pl.semaphore_signal(barrier, inc=1, device_id=peer, device_id_type=DEVICE)

    def send(src, dst, kind, arrived, peer):
        pltpu.make_async_remote_copy(
            src_ref=src, dst_ref=dst, send_sem=send_sem.at[kind], recv_sem=arrived,
            device_id=peer, device_id_type=DEVICE,
        ).start()

    def await_bytes(ref, sem):
        pltpu.make_async_copy(ref, ref, sem).wait()

    def half(i):
        return pl.ds(pl.multiple_of(i * HALF, HALF), HALF)

    def share(i):
        return pl.ds(pl.multiple_of(i * SHARE, SHARE), SHARE)

    def project(k):
        load_b[k].wait()
        part = jnp.dot(a_v[...], b_v[:, columns(k)], preferred_element_type=jnp.float32)
        p_v[k] = bf16(part)
        p32_v[k] = part
        if k == 0:
            pl.semaphore_wait(barrier, len(peers))
        send(p_v.at[k, half(1 - c)], r0_v.at[k], 0, pair_r.at[k], {"c": 1 - c})

    def pair_sum(k):
        await_bytes(r0_v.at[k], pair_r.at[k])
        total = p32_v[k, half(c)] + f32(r0_v[k])
        q_v[k] = bf16(total)
        q32_v[k] = total
        for o in (2, 1, 3):
            to = shifted("x", o)
            send(q_v.at[k, share(to)], r1_v.at[k, o - 1], 1, rs_r.at[k], {"x": to})

    own_rows = share(4 * c + x)

    def token_share(k):
        await_bytes(r1_v.at[k], rs_r.at[k])
        total = q32_v[k, share(x)]
        for o in range(3):
            total = total + f32(r1_v[k, o])
        t_v[k, own_rows] = bf16(total)
        for o in (2, 1, 3):
            rows = t_v.at[k, own_rows]
            send(rows, rows, 2, ag_r.at[k], {"x": shifted("x", o)})

    def join(k):
        await_bytes(r1_v.at[k], ag_r.at[k])
        send(t_v.at[k, half(c)], t_v.at[k, half(c)], 3, join_r.at[k], {"c": 1 - c})

    def parts_of(k):
        return range(SPLIT * k, SPLIT * (k + 1))

    def route(j):
        axes = ("y", "z") if j % 2 == 0 else ("z", "y")
        return axes + ((1, -1) if (j // 2) % 2 == 0 else (-1, 1))

    def gradient(k):
        await_bytes(t_v.at[k, half(c)], join_r.at[k])
        total = jnp.dot(gt_v[...], t_v[k], preferred_element_type=jnp.float32)
        for i, j in enumerate(parts_of(k)):
            axis, _, far, _ = route(j)
            piece = total[:, PART * i : PART * (i + 1)]
            if axis == "y":
                r32_v[j] = piece.reshape(8, 128, PART)
                r_v[j] = bf16(piece).reshape(8, 128, PART)
            else:
                for y in range(8):
                    rows = piece[128 * y : 128 * y + 128].reshape(8, 16, PART)
                    r32_v[j, :, pl.ds(16 * y, 16)] = rows
                    r_v[j, :, pl.ds(16 * y, 16)] = bf16(rows)
        for j in parts_of(k):
            axis, _, far, near = route(j)
            send(r_v.at[j, shifted(axis, 4)], in_v.at[j, 2], 4, in_r.at[j], {axis: shifted(axis, 2 * far)})
            for i, d in enumerate((far, near)):
                to = {axis: shifted(axis, d)}
                send(r_v.at[j, shifted(axis, 3 * d)], in_v.at[j, i], 4, in_r.at[j], to)
        for j in parts_of(k):
            axis, _, far, near = route(j)
            for i, d in enumerate((far, near)):
                to = shifted(axis, d)
                send(r_v.at[j, to], end_v.at[j, i], 4, end_r.at[j], {axis: to})

    def jump(k):
        for j in parts_of(k):
            await_bytes(in_v.at[j], in_r.at[j])
            axis, _, far, near = route(j)
            for i, d in enumerate((far, near)):
                to = shifted(axis, 2 * d)
                total = r32_v[j, to] + f32(in_v[j, i])
                if d == far:
                    total = total + f32(in_v[j, 2])
                hop_v[j, i] = bf16(total)
                send(hop_v.at[j, i], end_v.at[j, 2 + i], 5, end_r.at[j], {axis: to})

    def first_sum(k):
        for j in parts_of(k):
            await_bytes(end_v.at[j], end_r.at[j])
            axis, axis2, _, _ = route(j)
            total = r32_v[j, at[axis]]
            for i in range(4):
                total = total + f32(end_v[j, i])
            total = total.reshape(8, OWNED, PART)
            s_v[j] = bf16(total)
            s32_v[j] = total
            for o in (4, 3, 5, 2, 6, 1, 7):
                to = shifted(axis2, o)
                send(s_v.at[j, to], u_v.at[j, o - 1], 6, two_r.at[j], {axis2: to})

    def moments(k):
        me = 2 * x + c
        for i, j in enumerate(parts_of(k)):
            await_bytes(u_v.at[j], two_r.at[j])
            cols = pl.ds(j * PART, PART)
            reduced = s32_v[j, at[route(j)[1]]]
            for o in range(7):
                reduced = reduced + f32(u_v[j, o])
            new_first = beta_first * m1_v[:, cols] + (1.0 - beta_first) * reduced
            new_second = beta_second * m2_v[:, cols] + (1.0 - beta_second) * reduced * reduced
            first_out[:, cols] = new_first
            second_out[:, cols] = new_second
            bias_first = 1.0 - beta_first**STEP
            bias_second = 1.0 - beta_second**STEP
            normed = new_first / bias_first / (jnp.sqrt(new_second / bias_second) + epsilon)
            n_v[k, me, :, pl.ds(i * PART, PART)] = bf16(normed)
        for peer in mp_peers:
            send(n_v.at[k, me], n_v.at[k, me], 7, norm_r.at[k], peer)

    def expand(k):
        await_bytes(n_v.at[k, pl.ds(0, 7)], norm_r.at[k])
        stacked = n_v[k].reshape(8 * OWNED, WIDE)
        part = lax.dot_general(
            stacked, b_v[:, columns(k)], (((1,), (1,)), ((), ())), preferred_element_type=jnp.float32
        )
        if k == 0:
            full_v[...] = part
        elif k < CHUNKS - 1:
            full_v[...] += part
        else:
            update_out[...] = bf16(full_v[...] + part).reshape(8, OWNED, FEATURES)

    stages = (project, pair_sum, token_share, join, gradient, jump, first_sum, moments, expand)
    plan = sorted(
        (STAGE_AT[s] + k * STAGE_GAP[s], s, k) for s in range(len(stages)) for k in range(CHUNKS)
    )
    load_a.wait()
    turned = False
    for _, s, k in plan:
        if s == 2 and not turned:
            load_g.wait()
            gt_v[...] = g_v[...].T
            load_m1.wait()
            load_m2.wait()
            turned = True
        stages[s](k)
    gone = (
        r0_v, r1_v, r1_v, r0_v, r_v.at[:, pl.ds(0, 5)], hop_v, u_v, n_v.at[:, pl.ds(0, 7)],
    )
    for kind, ref in enumerate(gone):
        await_bytes(ref, send_sem.at[kind])


def write_out(first_v, second_v, update_v, first_hbm, second_hbm, update_hbm, sem):
    pairs = ((update_v, update_hbm), (first_v, first_hbm), (second_v, second_hbm))
    copies = [pltpu.make_async_copy(src, dst, sem.at[i]) for i, (src, dst) in enumerate(pairs)]
    for copy in copies:
        copy.start()
    for copy in copies:
        copy.wait()


def on_device(activations, out_grads, basis, moment1, moment2):
    def vmem(*shape, dtype=jnp.bfloat16):
        return pltpu.VMEM(shape, dtype)

    wide = jnp.float32
    sems = pltpu.SemaphoreType.DMA
    n, m = CHUNKS, PARTS
    counts = (4 + n, 8, n, n, n, n, m, m, m, n)
    in_hbm = pl.BlockSpec(memory_space=pltpu.HBM)
    in_vmem = pl.BlockSpec(memory_space=pltpu.VMEM)
    out_shape = (
        jax.ShapeDtypeStruct((OWNED, RANK), jnp.float32),
        jax.ShapeDtypeStruct((OWNED, RANK), jnp.float32),
        jax.ShapeDtypeStruct((8, OWNED, FEATURES), jnp.bfloat16),
    )
    results = pl.pallas_call(
        kernel,
        out_shape=out_shape,
        in_specs=[in_hbm] * 5,
        out_specs=(in_vmem,) * 3,
        scratch_shapes=[
            vmem(TOKENS, FEATURES),
            vmem(TOKENS, OUTS),
            vmem(FEATURES, RANK),
            vmem(OWNED, RANK, dtype=wide),
            vmem(OWNED, RANK, dtype=wide),
            vmem(OUTS, TOKENS),
            vmem(n, TOKENS, WIDE),
            vmem(n, TOKENS, WIDE, dtype=wide),
            vmem(n, HALF, WIDE),
            vmem(n, HALF, WIDE),
            vmem(n, HALF, WIDE, dtype=wide),
            vmem(n, 3, SHARE, WIDE),
            vmem(n, TOKENS, WIDE),
            vmem(m, 8, 128, PART),
            vmem(m, 8, 128, PART, dtype=wide),
            vmem(m, 2, 128, PART),
            vmem(m, 3, 128, PART),
            vmem(m, 4, 128, PART),
            vmem(m, 8, OWNED, PART),
            vmem(m, 8, OWNED, PART, dtype=wide),
            vmem(m, 7, OWNED, PART),
            vmem(n, 8, OWNED, WIDE),
            vmem(8 * OWNED, FEATURES, dtype=wide),
        ]
        + [sems((count,)) for count in counts],
        compiler_params=pltpu.CompilerParams(
            collective_id=0, has_side_effects=True, vmem_limit_bytes=55060 * 1024
        ),
        name="projected_adam",
    )(activations, out_grads, basis, moment1, moment2)
    return pl.pallas_call(
        write_out,
        out_shape=out_shape,
        in_specs=[in_vmem] * 3,
        out_specs=(in_hbm,) * 3,
        scratch_shapes=[sems((3,))],
        compiler_params=pltpu.CompilerParams(vmem_limit_bytes=1024 * 1024),
        name="write_out",
    )(*results)


def solution(mesh):
    finer = Mesh(mesh.devices.reshape(8, 8, 4, 2), ("y", "z", "x", "c"))
    dp, mp, owners = ("y", "z"), ("x", "c"), ("x", "c", "y", "z")
    in_specs = (P(dp, mp), P(dp, mp), P(mp, None), P(owners, None), P(owners, None))
    out_specs = (P(owners, None), P(owners, None), P(None, dp, mp))
    return jax.shard_map(
        on_device, mesh=finer, in_specs=in_specs, out_specs=out_specs, check_vma=False
    )
```

time: 78.8 us -> 58.7 us (0.74)
  Pallas kernels: 70.1 us -> 57 us
  local copies, waits for them, and re-layouts: 7.67 us -> 0.94 us
    pallas_call x1 -> x2, Pallas kernels: 70.1 us -> 57 us  [the longest x1 56.2 us: on_device(): pl.pallas_call(kernel, out_shape=out_shape, in_specs=[in_hbm] * 5, out_sp...]
    unnamed x13 -> x2, local copies, waits for them, and re-layouts: 7.67 us -> 0.94 us
where the time goes in v2:
time: 58.7 us; the launch traced here: 58.6 us
  Pallas kernels  57 us (97%)
  local copies, waits for them, and re-layouts  0.94 us (2%)
  between operations  0.65 us (1%)
    pallas_call x1, Pallas kernels, on_device(): pl.pallas_call(kernel, out_shape=out_shape, in_specs=[in_hbm] * 5, out_sp...  56.2 us

profile of v2, /device:TPU:1, one launch (start us, length us, event | category | flops | bytes accessed | tf_op | source)
XLA Modules:
  0.0 58.6 jit_solution(11391832342806134283)
XLA Ops:
  0.6 56.2 %projected_adam.1 = (f32[16,1024]{1,0:T(8,128)S(1)}, f32[16,1024]{1,0:T(8,128)S(1)}, bf16[8,16,1024]{2,1,0:T(8,128)(2,1)}) custom-call(bf16[512,1024]{1,0:T(8,128)(2,1)} %a_hbm.1, bf16[512,1024]{1,0:T(8,128)(2,1)} %g_hbm.1, bf16[1024,1024]{1,0:T(8,128)(2,1)} %b_hbm.1, f32[16,1024]{1,0:T(8,128)} %m1_hbm.1, f32[16,1024]{1,0:T(8,128)} %m2_hbm.1), custom_call_target="tpu_custom_call" | custom-call | tf_op jit(solution)/shard_map/projected_adam/pallas_call | solution.py:259
  56.9 0.0 copy-start
  56.9 0.9 %copy-done = bf16[8,16,1024]{2,1,0:T(8,128)(2,1)S(1)} copy-done((bf16[8,16,1024]{2,1,0:T(8,128)(2,1)S(1)}, bf16[8,16,1024]{2,1,0:T(8,128)(2,1)}, u32[]{:S(2)}) %copy-start) | copy-done | bytes 262168
  57.8 0.8 %write_out.1 = (f32[16,1024]{1,0:T(8,128)}, f32[16,1024]{1,0:T(8,128)}, bf16[8,16,1024]{2,1,0:T(8,128)(2,1)}) custom-call(f32[16,1024]{1,0:T(8,128)S(1)} %get-tuple-element.6.first_v, f32[16,1024]{1,0:T(8,128)S(1)} %get-tuple-element.7.second_v, bf16[8,16,1024]{2,1,0:T(8,128)(2,1)S(1)} %copy-done), custom_call_target="tpu_custom_call" | custom-call | tf_op jit(solution)/shard_map/write_out/pallas_call | solution.py:295
Async XLA Ops:
  56.9 1.0 %copy-start = (bf16[8,16,1024]{2,1,0:T(8,128)(2,1)S(1)}, bf16[8,16,1024]{2,1,0:T(8,128)(2,1)}, u32[]{:S(2)}) copy-start(bf16[8,16,1024]{2,1,0:T(8,128)(2,1)} %get-tuple-element.8.update_v) | copy-start | bytes 786436

commit v3 on v2

--- a/solution.py
+++ b/solution.py
@@ -23,8 +23,10 @@
 SHARE = TOKENS // 8
 OWNED = 16
 
-STAGE_AT = (0.0, 2.2, 7.5, 13.0, 15.5, 21.0, 28.0, 33.0, 37.0)
-STAGE_GAP = (1.4, 1.6, 2.8, 2.8, 2.8, 3.0, 3.0, 3.0, 3.0)
+ORDER = (
+    (0, 0), (0, 1), (1, 0), (1, 1), (2, 0), (2, 1), (3, 0), (4, 0), (3, 1),
+    (4, 1), (5, 0), (5, 1), (6, 0), (6, 1), (7, 0), (7, 1), (8, 0), (8, 1),
+)
 
 
 def f32(value):
@@ -37,7 +39,7 @@
 
 def kernel(
     a_hbm, g_hbm, b_hbm, m1_hbm, m2_hbm,
-    first_out, second_out, update_out,
+    first_out, second_out, up0, up1, up2, up3,
     a_v, g_v, b_v, m1_v, m2_v, gt_v,
     p_v, p32_v, r0_v, q_v, q32_v, r1_v, t_v, r_v, r32_v, hop_v, in_v, end_v,
     s_v, s32_v, u_v, n_v, full_v,
@@ -209,12 +211,12 @@
         elif k < CHUNKS - 1:
             full_v[...] += part
         else:
-            update_out[...] = bf16(full_v[...] + part).reshape(8, OWNED, FEATURES)
+            whole = bf16(full_v[...] + part).reshape(8, OWNED, FEATURES)
+            for i, out in enumerate((up0, up1, up2, up3)):
+                out[...] = whole[2 * i : 2 * i + 2]
 
     stages = (project, pair_sum, token_share, join, gradient, jump, first_sum, moments, expand)
-    plan = sorted(
-        (STAGE_AT[s] + k * STAGE_GAP[s], s, k) for s in range(len(stages)) for k in range(CHUNKS)
-    )
+    plan = [(0, s, k) for s, k in ORDER]
     load_a.wait()
     turned = False
     for _, s, k in plan:
@@ -232,8 +234,10 @@
         await_bytes(ref, send_sem.at[kind])
 
 
-def write_out(first_v, second_v, update_v, first_hbm, second_hbm, update_hbm, sem):
-    pairs = ((update_v, update_hbm), (first_v, first_hbm), (second_v, second_hbm))
+def write_out(first_v, second_v, *rest):
+    pieces, (first_hbm, second_hbm, update_hbm, sem) = rest[:4], rest[4:]
+    pairs = [(piece, update_hbm.at[pl.ds(2 * i, 2)]) for i, piece in enumerate(pieces)]
+    pairs += [(first_v, first_hbm), (second_v, second_hbm)]
     copies = [pltpu.make_async_copy(src, dst, sem.at[i]) for i, (src, dst) in enumerate(pairs)]
     for copy in copies:
         copy.start()
@@ -258,9 +262,9 @@
     )
     results = pl.pallas_call(
         kernel,
-        out_shape=out_shape,
+        out_shape=out_shape[:2] + (jax.ShapeDtypeStruct((2, OWNED, FEATURES), jnp.bfloat16),) * 4,
         in_specs=[in_hbm] * 5,
-        out_specs=(in_vmem,) * 3,
+        out_specs=(in_vmem,) * 6,
         scratch_shapes=[
             vmem(TOKENS, FEATURES),
             vmem(TOKENS, OUTS),
@@ -288,16 +292,16 @@
         ]
         + [sems((count,)) for count in counts],
         compiler_params=pltpu.CompilerParams(
-            collective_id=0, has_side_effects=True, vmem_limit_bytes=55060 * 1024
+            collective_id=0, has_side_effects=True, vmem_limit_bytes=54800 * 1024
         ),
         name="projected_adam",
     )(activations, out_grads, basis, moment1, moment2)
     return pl.pallas_call(
         write_out,
         out_shape=out_shape,
-        in_specs=[in_vmem] * 3,
+        in_specs=[in_vmem] * 6,
         out_specs=(in_hbm,) * 3,
-        scratch_shapes=[sems((3,))],
+        scratch_shapes=[sems((6,))],
         compiler_params=pltpu.CompilerParams(vmem_limit_bytes=1024 * 1024),
         name="write_out",
     )(*results)

time: 58.7 us -> 57.1 us (0.973)
  local copies, waits for them, and re-layouts: 0.94 us -> 0 us
  Pallas kernels: 57 us -> 56.3 us
    unnamed x2 -> x0, local copies, waits for them, and re-layouts: 0.94 us -> none
    pallas_call x2, Pallas kernels: 57 us -> 56.3 us  [the longest x1 55.5 us: on_device(): pl.pallas_call(kernel, out_shape=out_shape[:2] + (jax.ShapeDtypeStruct((2...]
where the time goes in v3:
time: 57.1 us; the launch traced here: 57 us
  Pallas kernels  56.3 us (99%)
  between operations  0.64 us (1%)
    pallas_call x1, Pallas kernels, on_device(): pl.pallas_call(kernel, out_shape=out_shape[:2] + (jax.ShapeDtypeStruct((2...  55.5 us

profile of v3, /device:TPU:1, one launch (start us, length us, event | category | flops | bytes accessed | tf_op | source)
XLA Modules:
  0.0 57.0 jit_solution(11266682397736814629)
XLA Ops:
  0.6 55.5 %projected_adam.1 = (f32[16,1024]{1,0:T(8,128)S(1)}, f32[16,1024]{1,0:T(8,128)S(1)}, bf16[2,16,1024]{2,1,0:T(8,128)(2,1)S(1)}, bf16[2,16,1024]{2,1,0:T(8,128)(2,...) custom-call(bf16[512,1024]{1,0:T(8,128)(2,1)} %a_hbm.1, bf16[512,1024]{1,0:T(8,128)(2,1)} %g_hbm.1, ...), custom_call_target="tpu_custom_call" | custom-call | tf_op jit(solution)/shard_map/projected_adam/pallas_call | solution.py:263
  56.2 0.8 %write_out.1 = (f32[16,1024]{1,0:T(8,128)}, f32[16,1024]{1,0:T(8,128)}, bf16[8,16,1024]{2,1,0:T(8,128)(2,1)}) custom-call(f32[16,1024]{1,0:T(8,128)S(1)} %get-tuple-element.9.first_v, f32[16,1024]{1,0:T(8,128)S(1)} %get-tuple-element.10.second_v, bf16[2,16,1024]{2,1,0:T(8,128)(2,1)S(1)} %get-tuple-element.11.rest_0_, ...), custom_call_target="tpu_custom_call" | custom-call | tf_op jit(solution)/shard_map/write_out/pallas_call | solution.py:299

commit v4 on v3

--- a/solution.py
+++ b/solution.py
@@ -66,7 +66,7 @@
     load_m2 = load(m2_hbm, m2_v, 3 + CHUNKS)
 
     mp_peers = [
-        {"x": shifted("x", dx), "c": shifted("c", dc)} for dx in range(4) for dc in range(2) if dx or dc
+        {"x": shifted("x", dx), "c": shifted("c", dc)} for dx in (1, 3, 2, 0) for dc in range(2) if dx or dc
     ]
     barrier = pltpu.get_barrier_semaphore()
     peers = mp_peers + [{axis: shifted(axis, o)} for axis in ("y", "z") for o in range(1, 8)]
@@ -102,7 +102,7 @@
         total = p32_v[k, half(c)] + f32(r0_v[k])
         q_v[k] = bf16(total)
         q32_v[k] = total
-        for o in (2, 1, 3):
+        for o in (1, 3, 2):
             to = shifted("x", o)
             send(q_v.at[k, share(to)], r1_v.at[k, o - 1], 1, rs_r.at[k], {"x": to})
 
@@ -114,7 +114,7 @@
         for o in range(3):
             total = total + f32(r1_v[k, o])
         t_v[k, own_rows] = bf16(total)
-        for o in (2, 1, 3):
+        for o in (1, 3, 2):
             rows = t_v.at[k, own_rows]
             send(rows, rows, 2, ag_r.at[k], {"x": shifted("x", o)})
 

time: 57.1 us -> 57.1 us (level)
  no operation moved by 1% of the time
where the time goes in v4:
time: 57.1 us; the launch traced here: 56.9 us
  Pallas kernels  56.3 us (99%)
  between operations  0.64 us (1%)
    pallas_call x1, Pallas kernels, on_device(): pl.pallas_call(kernel, out_shape=out_shape[:2] + (jax.ShapeDtypeStruct((2...  55.5 us

profile of v4, /device:TPU:1, one launch (start us, length us, event | category | flops | bytes accessed | tf_op | source)
XLA Modules:
  0.0 56.9 jit_solution(6954177060757281933)
XLA Ops:
  0.6 55.5 %projected_adam.1 = (f32[16,1024]{1,0:T(8,128)S(1)}, f32[16,1024]{1,0:T(8,128)S(1)}, bf16[2,16,1024]{2,1,0:T(8,128)(2,1)S(1)}, bf16[2,16,1024]{2,1,0:T(8,128)(2,...) custom-call(bf16[512,1024]{1,0:T(8,128)(2,1)} %a_hbm.1, bf16[512,1024]{1,0:T(8,128)(2,1)} %g_hbm.1, ...), custom_call_target="tpu_custom_call" | custom-call | tf_op jit(solution)/shard_map/projected_adam/pallas_call | solution.py:263
  56.1 0.8 %write_out.1 = (f32[16,1024]{1,0:T(8,128)}, f32[16,1024]{1,0:T(8,128)}, bf16[8,16,1024]{2,1,0:T(8,128)(2,1)}) custom-call(f32[16,1024]{1,0:T(8,128)S(1)} %get-tuple-element.9.first_v, f32[16,1024]{1,0:T(8,128)S(1)} %get-tuple-element.10.second_v, bf16[2,16,1024]{2,1,0:T(8,128)(2,1)S(1)} %get-tuple-element.11.rest_0_, ...), custom_call_target="tpu_custom_call" | custom-call | tf_op jit(solution)/shard_map/write_out/pallas_call | solution.py:299
